TPU v7x, 32 devices: a whole 2x2x4 slice. The times are simulated.
32 devices in a mesh: dp: 4 (over y, x), segment: 2 (over core), band: 4 (over z).
Axes of the slice: x: 2, y: 2, z: 4, core: 2. Of those that a mesh axis runs over, the one named last changes fastest.
Arguments:
- fields: bfloat16 [4, 2, 32, 16, 512], P('dp', None, 'band'), may hold values from -6 to 6
- cell_mask: int32 [4, 2, 32, 16], P('dp', None, 'band'), may hold values 0 or 1
- merge_weight: bfloat16 [2, 1024, 512], P('segment', 'dp'), may hold values from -0.1875 to 0.1875
- qkv_weight: bfloat16 [2, 512, 1536], P('segment', 'dp')
- out_weight: bfloat16 [2, 512, 512], P('segment', 'dp'), may hold values from -1 to 1
- norm_gain: bfloat16 [2, 512], P('segment', 'dp'), may hold values from 0.099609375 to 1.8984375
- out_cotangent: bfloat16 [4, 2, 32, 16, 512], P('dp', None, 'band'), may hold values from -6 to 6
Outputs:
- section_out: bfloat16 [2, 4, 2, 32, 16, 512], P('segment', 'dp', None, 'band')
- merge_grad: float32 [2, 1024, 512], P('segment', 'dp')
- qkv_grad: float32 [2, 512, 1536], P('segment', 'dp')
- out_grad: float32 [2, 512, 512], P('segment', 'dp')
- gain_grad: float32 [2, 512], P('segment', 'dp')
Inputs may be any that keep to these rules, and one draw needn't show every extreme that they name: `cell_mask`: 1 marks a cell whose keys may be attended.
All inputs are finite; a program needn't handle non-finite values. No bound on the sum of `cell_mask` on one device may be relied on, other than what follows from the above.
Results may differ from a plain program's by a relative error of at most 0.03.
Values may be sent and summed in bfloat16 or wider, within the bound.
No kernel may reach another device: no remote copies, remote signals or barrier semaphores. Data moves between devices by JAX's collectives and lax.ppermute only.
A program may use at most 128 MiB of HBM per device.

v0:
```python
import jax
import jax.numpy as jnp
from jax import lax
from jax.sharding import PartitionSpec as P

HEADS = 8
WH = 8
WW = 16
SH = 4
SW = 8
EPSILON = 1e-05
MASKED = -1e30


def padded(shard, sides, width):
    for axis, dim in sides:
        size, length = (lax.axis_size(axis), shard.shape[dim])
        up = [(i, (i + 1) % size) for i in range(size - 1)]
        down = [(j, i) for i, j in up]
        last = lax.slice_in_dim(shard, length - width, length, axis=dim)
        first = lax.slice_in_dim(shard, 0, width, axis=dim)
        before = lax.ppermute(last, axis, up)
        after = lax.ppermute(first, axis, down)
        shard = jnp.concatenate([before, shard, after], axis=dim)
    return shard


def normalize(update):
    average = jnp.mean(update, axis=-1, keepdims=True)
    centered = update - average
    spread = jnp.mean(centered * centered, axis=-1, keepdims=True)
    inverse = lax.rsqrt(spread + EPSILON)
    return (centered * inverse, inverse)


def window_pattern(lon_count):
    query_index = jnp.arange(WH * lon_count, dtype=jnp.int32)
    key_index = jnp.arange(2 * WH * lon_count, dtype=jnp.int32)
    query_row = query_index // lon_count
    query_col = query_index % lon_count
    key_row = key_index // lon_count
    key_col = key_index % lon_count
    lat_same = ((query_row + SH) // WH)[:, None] == (key_row // WH)[None, :]
    lon_same = ((query_col + SW) // WW)[:, None] == ((key_col + SW) // WW)[None, :]
    self_key = ((query_row + SH)[:, None] == key_row[None, :]) & (
        query_col[:, None] == key_col[None, :]
    )
    return (lat_same & lon_same, self_key)


def attend(queries, keyvals, usable):
    row_count, lon_count, feature = queries.shape
    blocks = row_count // WH
    head_dim = feature // HEADS
    query_blocks = queries.reshape(blocks, WH * lon_count, HEADS, head_dim)
    kv_blocks = keyvals.reshape(blocks + 1, WH * lon_count, 2, HEADS, head_dim)
    key_pairs = jnp.concatenate([kv_blocks[:-1], kv_blocks[1:]], axis=1)
    use_blocks = usable.reshape(blocks + 1, WH * lon_count)
    use_pairs = jnp.concatenate([use_blocks[:-1], use_blocks[1:]], axis=1)
    inside, self_key = window_pattern(lon_count)
    allowed = inside[None] & (use_pairs[:, None, :] | self_key[None])
    scores = jnp.einsum(
        "nqhd,nkhd->nhqk", query_blocks, key_pairs[:, :, 0], preferred_element_type=jnp.float32
    ) * head_dim ** (-0.5)
    scores = jnp.where(allowed[:, None], scores, MASKED)
    highest = jnp.max(scores, axis=-1, keepdims=True)
    weights = jnp.exp(scores - highest)
    attn_prob = (weights / jnp.sum(weights, axis=-1, keepdims=True)).astype(jnp.bfloat16)
    mixture = jnp.einsum(
        "nhqk,nkhd->nqhd", attn_prob, key_pairs[:, :, 1], preferred_element_type=jnp.float32
    )
    return mixture.reshape(row_count, lon_count, feature).astype(jnp.bfloat16)


def guarded(active, function, operands):

    def skipped(values):
        return jax.tree.map(jnp.zeros_like, function(values))

    return lax.cond(active, function, skipped, operands)


def project(joined, merge_full, qkv_full, gain_full):
    update = jnp.einsum("rwj,jd->rwd", joined, merge_full, preferred_element_type=jnp.float32)
    normed, inverse = normalize(update)
    hidden = (normed * gain_full.astype(jnp.float32)).astype(jnp.bfloat16)
    projected = jnp.einsum("rwd,de->rwe", hidden, qkv_full, preferred_element_type=jnp.float32)
    feature = update.shape[-1]
    queries = projected[..., :feature].astype(jnp.bfloat16)
    keyvals = projected[..., feature:].astype(jnp.bfloat16)
    return (update, normed, inverse, hidden, queries, keyvals)


def section_forward(active, joined, usable, merge_full, qkv_full, gain_full, out_full):
    update, normed, inverse, hidden, queries, own_keys = guarded(
        active, lambda rows_own: project(rows_own, merge_full, qkv_full, gain_full), joined
    )
    keyvals = padded(own_keys, (("band", 0),), SH)

    def finish(operands):
        update_in, query_in, keyval_in, usable_in = operands
        mixture = attend(query_in, keyval_in, usable_in)
        result = (
            update_in
            + jnp.einsum("rwd,de->rwe", mixture, out_full, preferred_element_type=jnp.float32)
        ).astype(jnp.bfloat16)
        return (mixture, result)

    mixture, result = guarded(active, finish, (update, queries, keyvals, usable))
    return (result, (joined, normed, inverse, hidden, queries, keyvals, mixture))


def attend_back(out_full, operands):
    grad_out, queries, keyvals, mixture, usable = operands
    grad_mixture = jnp.einsum(
        "rwe,de->rwd", grad_out, out_full, preferred_element_type=jnp.float32
    ).astype(jnp.bfloat16)
    unused, pull_back = jax.vjp(
        lambda query_in, keyval_in: attend(query_in, keyval_in, usable), queries, keyvals
    )
    grad_query, grad_keyval = pull_back(grad_mixture)
    grad_outw = jnp.einsum("rwd,rwe->de", mixture, grad_out, preferred_element_type=jnp.float32)
    return (grad_query, grad_keyval, grad_outw)


def fold_rims(grad_keyval, row_count):
    rim_rows = jnp.concatenate([grad_keyval[:SH], grad_keyval[SH + row_count :]], axis=0)
    returned = padded(rim_rows, (("band", 0),), SH)
    own_part = grad_keyval[SH : SH + row_count].astype(jnp.float32)
    return jnp.concatenate(
        [
            own_part[:SH] + returned[:SH].astype(jnp.float32),
            own_part[SH : row_count - SH],
            own_part[row_count - SH :] + returned[3 * SH :].astype(jnp.float32),
        ],
        axis=0,
    ).astype(jnp.bfloat16)


def back_core(qkv_full, gain_full, grad_query, grad_keyown, grad_out, normed, inverse):
    grad_proj = jnp.concatenate([grad_query, grad_keyown], axis=-1)
    grad_hidden = jnp.einsum("rwe,de->rwd", grad_proj, qkv_full, preferred_element_type=jnp.float32)
    grad_normed = grad_hidden * gain_full.astype(jnp.float32)
    grad_update = (
        grad_out.astype(jnp.float32)
        + inverse
        * (
            grad_normed
            - jnp.mean(grad_normed, axis=-1, keepdims=True)
            - normed * jnp.mean(grad_normed * normed, axis=-1, keepdims=True)
        )
    ).astype(jnp.bfloat16)
    return (grad_proj, grad_hidden, grad_update)


def body(fields, cell_mask, merge_weight, qkv_weight, out_weight, norm_gain, out_cotangent):
    merge_rows, qkv_rows, out_rows, gain_rows = (
        lax.all_gather(merge_weight, "dp", axis=1, tiled=True),
        lax.all_gather(qkv_weight, "dp", axis=1, tiled=True),
        lax.all_gather(out_weight, "dp", axis=1, tiled=True),
        lax.all_gather(norm_gain, "dp", axis=1, tiled=True),
    )
    merge_full = merge_rows[0]
    qkv_full = qkv_rows[0]
    inputs = fields[0]
    cotangent = out_cotangent[0]
    micro_count, row_count, lon_count, feature = inputs.shape
    mask_ext = padded(cell_mask[0], (("band", 1),), SH)
    usable_ext = mask_ext == 1
    section_count = lax.axis_size("segment")
    half_count = section_count // 2
    section_rank = lax.axis_index("segment")
    merge_all, qkv_all, out_all, gain_all = (
        lax.all_gather(merge_rows, "segment", axis=0, tiled=True),
        lax.all_gather(qkv_rows, "segment", axis=0, tiled=True),
        lax.all_gather(out_rows, "segment", axis=0, tiled=True),
        lax.all_gather(gain_rows, "segment", axis=0, tiled=True),
    )
    local_count = micro_count // section_count
    always = jnp.array(True)
    shipped = [[] for index in range(section_count)]
    pick = section_rank * local_count + 0
    inputs_now = lax.dynamic_index_in_dim(inputs, pick, 0, keepdims=False)
    cotangent_now = lax.dynamic_index_in_dim(cotangent, pick, 0, keepdims=False)
    usable_now = lax.dynamic_index_in_dim(usable_ext, pick, 0, keepdims=False)
    outputs = []
    records = []
    for index in range(section_count):
        chain_in = inputs_now if index == 0 else outputs[index - 1]
        side_in = inputs_now if index < half_count else outputs[section_count - 1 - index]
        joined = jnp.concatenate([chain_in, side_in], axis=-1)
        result, record = section_forward(
            always,
            joined,
            usable_now,
            merge_all[index],
            qkv_all[index],
            gain_all[index],
            out_all[index],
        )
        outputs.append(result)
        records.append(record)
    flows = [None] * section_count
    for index in range(section_count - 1, -1, -1):
        grad_out = (
            cotangent_now if index == section_count - 1 else flows[index].astype(jnp.bfloat16)
        )
        joined, normed, inverse, hidden, queries, keyvals, mixture = records[index]
        grad_query, grad_keyval, unused = attend_back(
            out_all[index], (grad_out, queries, keyvals, mixture, usable_now)
        )
        grad_keyown = fold_rims(grad_keyval, row_count)
        grad_proj, unused, grad_update = back_core(
            qkv_all[index], gain_all[index], grad_query, grad_keyown, grad_out, normed, inverse
        )
        grad_joined = jnp.einsum(
            "rwd,jd->rwj", grad_update, merge_all[index], preferred_element_type=jnp.float32
        )
        grad_chain = grad_joined[..., :feature].astype(jnp.bfloat16).astype(jnp.float32)
        grad_side = grad_joined[..., feature:].astype(jnp.bfloat16).astype(jnp.float32)
        if index > 0:
            flows[index - 1] = grad_chain
        if index >= half_count:
            target = section_count - 1 - index
            flows[target] = flows[target] + grad_side
        shipped[index].append(
            (outputs[index], joined, grad_update, hidden, grad_proj, mixture, grad_out)
        )
    packed = tuple(
        (
            jnp.stack([jnp.stack([shipped[index][0][field]]) for index in range(section_count)])
            for field in range(7)
        )
    )
    home = (
        lax.all_to_all(packed[0], "segment", split_axis=0, concat_axis=1, tiled=True),
        lax.all_to_all(packed[1], "segment", split_axis=0, concat_axis=1, tiled=True),
        lax.all_to_all(packed[2], "segment", split_axis=0, concat_axis=1, tiled=True),
        lax.all_to_all(packed[3], "segment", split_axis=0, concat_axis=1, tiled=True),
        lax.all_to_all(packed[4], "segment", split_axis=0, concat_axis=1, tiled=True),
        lax.all_to_all(packed[5], "segment", split_axis=0, concat_axis=1, tiled=True),
        lax.all_to_all(packed[6], "segment", split_axis=0, concat_axis=1, tiled=True),
    )
    joined_all, grad_update_all, hidden_all, grad_proj_all, mixture_all, grad_out_all = [
        part[0] for part in home[1:]
    ]
    grad_merge = jnp.einsum(
        "mrwj,mrwd->jd", joined_all, grad_update_all, preferred_element_type=jnp.float32
    )
    grad_qkv = jnp.einsum(
        "mrwd,mrwe->de", hidden_all, grad_proj_all, preferred_element_type=jnp.float32
    )
    grad_outw = jnp.einsum(
        "mrwd,mrwe->de", mixture_all, grad_out_all, preferred_element_type=jnp.float32
    )
    update_all = jnp.einsum(
        "mrwj,jd->mrwd", joined_all, merge_full, preferred_element_type=jnp.float32
    )
    normed_all, unused = normalize(update_all)
    grad_hidden_all = jnp.einsum(
        "mrwe,de->mrwd", grad_proj_all, qkv_full, preferred_element_type=jnp.float32
    )
    grad_gain = jnp.sum(grad_hidden_all * normed_all, axis=(0, 1, 2))
    grad_sums = (grad_merge, grad_qkv, grad_outw, grad_gain)
    section_home = home[0][None]
    merge_part_sum, qkv_part_sum, out_part_sum, gain_part_sum = (
        lax.psum_scatter(
            grad_sums[0][None].astype(jnp.bfloat16), "dp", scatter_dimension=1, tiled=True
        ).astype(jnp.float32),
        lax.psum_scatter(
            grad_sums[1][None].astype(jnp.bfloat16), "dp", scatter_dimension=1, tiled=True
        ).astype(jnp.float32),
        lax.psum_scatter(
            grad_sums[2][None].astype(jnp.bfloat16), "dp", scatter_dimension=1, tiled=True
        ).astype(jnp.float32),
        lax.psum_scatter(
            grad_sums[3][None].astype(jnp.bfloat16), "dp", scatter_dimension=1, tiled=True
        ).astype(jnp.float32),
    )
    merge_grad, qkv_grad, out_grad, gain_grad = (
        lax.psum(merge_part_sum.astype(jnp.bfloat16), "band").astype(jnp.float32),
        lax.psum(qkv_part_sum.astype(jnp.bfloat16), "band").astype(jnp.float32),
        lax.psum(out_part_sum.astype(jnp.bfloat16), "band").astype(jnp.float32),
        lax.psum(gain_part_sum.astype(jnp.bfloat16), "band").astype(jnp.float32),
    )
    return (section_home, merge_grad, qkv_grad, out_grad, gain_grad)


def solution(mesh):
    return jax.shard_map(
        body,
        mesh=mesh,
        in_specs=(
            P("dp", None, "band", None, None),
            P("dp", None, "band", None),
            P("segment", "dp", None),
            P("segment", "dp", None),
            P("segment", "dp", None),
            P("segment", "dp"),
            P("dp", None, "band", None, None),
        ),
        out_specs=(
            P("segment", "dp", None, "band", None, None),
            P("segment", "dp", None),
            P("segment", "dp", None),
            P("segment", "dp", None),
            P("segment", "dp"),
        ),
        check_vma=False,
    )
```

profile of v0, /device:TPU:0, one launch (start us, length us, event | category | flops | bytes accessed | tf_op | source)
XLA Modules:
  0.0 377.2 jit_solution(2174182986141230632)
XLA Ops:
  8.8 30.4 %all-gather.7.cloned.1.call-done = bf16[1,1024,512]{2,1,0:T(8,128)(2,1)} async-done(((bf16[1,256,512]{2,1,0:T(8,128)(2,1)}), bf16[1,1024,512]{2,1,0:T(8,128)(2,1)}) %all-gather.7.cloned.1.call-update) | async-done | bytes 1048592 | tf_op jit(solution)/shard_map/all_gather | solution.py:158
  39.2 32.6 %all-gather.11.cloned.1.call-done = bf16[1,512,1536]{2,1,0:T(8,128)(2,1)} async-done(((bf16[1,128,1536]{2,1,0:T(8,128)(2,1)}), bf16[1,512,1536]{2,1,0:T(8,128)(2,1)}) %all-gather.11.cloned.1.call-update) | async-done | bytes 1572880 | tf_op jit(solution)/shard_map/all_gather | solution.py:159
  73.2 4.5 %collective-permute-start.2 = (s32[2,4,16]{2,1,0:T(4,128)S(1)}, s32[2,4,16]{2,1,0:T(4,128)S(1)}, u32[]{:S(2)}, u32[]{:S(2)}) collective-permute-start(s32[2,4,16]{2,1,0:T(4,128)S(1)} %get-tuple-element.47), channel_id=1, source_target_pairs={{0,1},{1,2},{2,3},{4,5},{5,6},{6,7},{8,9},{9,10},{10,11},{12,13},{... | collective-permute-start | bytes 1544 | tf_op jit(solution)/shard_map/ppermute | solution.py:22
  77.8 10.6 %all_gather.30 = bf16[1,512,512]{2,1,0:T(8,128)(2,1)} all-gather(bf16[1,128,512]{2,1,0:T(8,128)(2,1)S(1)} %copy-done.33), channel_id=1, replica_groups=mesh['dp'=4,'segment'=2,'band'=4] {'dp'}, dimensions={1}, use_global_device_ids=true | all-gather | bytes 655360 | tf_op jit(solution)/shard_map/all_gather | solution.py:160
  88.5 7.1 %all_gather.26 = bf16[1,512]{1,0:T(2,128)(2,1)S(1)} all-gather(bf16[1,128]{1,0:T(2,128)(2,1)S(1)} %copy-done.44), channel_id=1, replica_groups=mesh['dp'=4,'segment'=2,'band'=4] {'dp'}, dimensions={1}, use_global_device_ids=true | all-gather | bytes 1280 | tf_op jit(solution)/shard_map/all_gather | solution.py:161
  95.6 1.8 all-gather
  98.5 1.6 fusion.133
  100.4 1.8 convolution_convert_fusion.1
  102.3 3.4 collective-permute-start
  107.0 3.3 all-gather.15.cloned.1.call-done
  117.3 1.4 fusion.23
  118.7 1.6 fusion.135
  125.8 3.4 collective-permute-start.4
  129.2 1.5 collective-permute-start.5
  131.2 1.4 collective-permute-done.4
  132.7 3.8 %collective-permute-done.5 = bf16[4,16,1024]{2,1,0:T(8,128)(2,1)S(1)} collective-permute-done((bf16[4,16,1024]{2,1,0:T(8,128)(2,1)S(1)}, bf16[4,16,1024]{2,1,0:T(8,128)(2,1)S(1)}, u32[]{:S(2)}, u32[]{:S(2)}) %collective-permute-start.5) | collective-permute-done | bytes 131104 | tf_op jit(solution)/shard_map/ppermute | solution.py:23
  136.5 1.7 pad_maximum_fusion.4
  144.3 1.7 fusion.19
  146.0 1.6 fusion.28
  149.3 4.1 %all-to-all-start.5 = ((bf16[2,1,8,16,512]{4,3,2,1,0:T(8,128)(2,1)}), bf16[2,1,8,16,512]{4,3,2,1,0:T(8,128)(2,1)}, u32[]{:S(2)}, u32[]{:S(2)}) async-start(bf16[2,1,8,16,512]{4,3,2,1,0:T(8,128)(2,1)} %pad_maximum_fusion.13), calls=%async_computation.7 | async-start | bytes 524288 | tf_op jit(solution)/shard_map/all_to_all | solution.py:241
  156.7 1.8 copy.63
  158.5 1.5 reshape.688
  161.1 3.4 collective-permute-start.6
  164.4 1.5 collective-permute-start.7
  167.8 4.1 %collective-permute-done.7 = bf16[4,16,1024]{2,1,0:T(8,128)(2,1)S(1)} collective-permute-done((bf16[4,16,1024]{2,1,0:T(8,128)(2,1)S(1)}, bf16[4,16,1024]{2,1,0:T(8,128)(2,1)S(1)}, u32[]{:S(2)}, u32[]{:S(2)}) %collective-permute-start.7) | collective-permute-done | bytes 131104 | tf_op jit(solution)/shard_map/ppermute | solution.py:23
  172.0 2.3 fusion.126
  178.3 1.7 fusion.29
  183.2 3.4 collective-permute-start.8
  189.1 4.4 %collective-permute-done.9 = bf16[4,16,1024]{2,1,0:T(8,128)(2,1)S(1)} collective-permute-done((bf16[4,16,1024]{2,1,0:T(8,128)(2,1)S(1)}, bf16[4,16,1024]{2,1,0:T(8,128)(2,1)S(1)}, u32[]{:S(2)}, u32[]{:S(2)}) %collective-permute-start.9) | collective-permute-done | bytes 131104 | tf_op jit(solution)/shard_map/ppermute | solution.py:23
  193.5 2.2 fusion.125
  196.0 3.9 %all_to_all.28 = bf16[2,1,8,16,512]{4,3,2,1,0:T(8,128)(2,1)S(1)} all-to-all(bf16[2,1,8,16,512]{4,3,2,1,0:T(8,128)(2,1)S(1)} %pad_maximum_fusion.14), channel_id=1, replica_groups=mesh['dp'=4,'segment'=2,'band'=4] {'segment'}, dimensions={0} | all-to-all | bytes 524288 | tf_op jit(solution)/shard_map/all_to_all | solution.py:242
  199.9 2.1 fusion.10
  203.0 3.5 all-to-all-start.1
  206.5 1.6 all-to-all-done.1
  208.2 3.9 %all_to_all.29 = bf16[2,1,8,16,512]{4,3,2,1,0:T(8,128)(2,1)S(1)} all-to-all(bf16[2,1,8,16,512]{4,3,2,1,0:T(8,128)(2,1)S(1)} %pad_maximum_fusion.11), channel_id=1, replica_groups=mesh['dp'=4,'segment'=2,'band'=4] {'segment'}, dimensions={0} | all-to-all | bytes 524288 | tf_op jit(solution)/shard_map/all_to_all | solution.py:238
  212.1 1.5 fusion.6
  214.4 3.4 all-to-all-start.3
  220.1 4.4 %all_to_all.30 = bf16[2,1,8,16,1536]{4,3,2,1,0:T(8,128)(2,1)S(1)} all-to-all(bf16[2,1,8,16,1536]{4,3,2,1,0:T(8,128)(2,1)S(1)} %pad_maximum_fusion), channel_id=1, replica_groups=mesh['dp'=4,'segment'=2,'band'=4] {'segment'}, dimensions={0} | all-to-all | bytes 1572864 | tf_op jit(solution)/shard_map/all_to_all | solution.py:240
  224.4 2.8 fusion.1
  230.3 26.1 %reduce-scatter.7.cloned.1.call-done = bf16[1,256,512]{2,1,0:T(8,128)(2,1)} async-done(((bf16[1,1024,512]{2,1,0:T(8,128)(2,1)}), bf16[1,256,512]{2,1,0:T(8,128)(2,1)}) %reduce-scatter.7.cloned.1.call-update) | async-done | bytes 262160 | tf_op jit(solution)/shard_map/reduce_scatter | solution.py:267
  256.3 34.2 %reduce-scatter.9.cloned.1.call-done = bf16[1,128,1536]{2,1,0:T(8,128)(2,1)} async-done(((bf16[1,512,1536]{2,1,0:T(8,128)(2,1)}), bf16[1,128,1536]{2,1,0:T(8,128)(2,1)}) %reduce-scatter.9.cloned.1.call-update) | async-done | bytes 393232 | tf_op jit(solution)/shard_map/reduce_scatter | solution.py:270
  291.0 3.9 %all_to_all.31 = bf16[2,1,8,16,512]{4,3,2,1,0:T(8,128)(2,1)S(1)} all-to-all(bf16[2,1,8,16,512]{4,3,2,1,0:T(8,128)(2,1)S(1)} %pad_maximum_fusion.10), channel_id=1, replica_groups=mesh['dp'=4,'segment'=2,'band'=4] {'segment'}, dimensions={0} | all-to-all | bytes 524288 | tf_op jit(solution)/shard_map/all_to_all | solution.py:236
  295.0 23.0 %reduce-scatter.13.cloned.1.call-done = bf16[128,1]{1,0:T(8,128)(2,1)} async-done(((bf16[512,1]{1,0:T(8,128)(2,1)}), bf16[128,1]{1,0:T(8,128)(2,1)}) %reduce-scatter.13.cloned.1.call-update) | async-done | bytes 272
  318.8 11.7 %psum.31 = bf16[1,128]{1,0:T(2,128)(2,1)S(1)} all-reduce(bf16[1,128]{1,0:T(2,128)(2,1)S(1)} %copy.77), channel_id=1, replica_groups=mesh['dp'=4,'segment'=2,'band'=4] {'band'}, use_global_device_ids=true, to_apply=%region_28.29 | all-reduce | flops 128 | bytes 512 | tf_op jit(solution)/shard_map/psum | solution.py:284
  331.0 33.2 %all-reduce.11.cloned.1.call-done = (bf16[1,256,512]{2,1,0:T(8,128)(2,1)}, bf16[1,128,1536]{2,1,0:T(8,128)(2,1)}, bf16[1,128,512]{2,1,0:T(8,128)(2,1)}) async-done(((bf16[1,256,512]{2,1,0:T(8,128)(2,1)}, bf16[1,128,1536]{2,1,0:T(8,128)(2,1)}, bf16[1,128,512]{2,1,0:T(8,128)(2,1)}), (bf16[1,256,512]{2,1,0:T(8,128)(2,1)}, bf16[1,128,1536]{2,1,0:T(8,128)(2,1)}, ...) | async-done | bytes 786448 | tf_op jit(solution)/shard_map/psum | solution.py:281
  364.3 1.8 convert_element_type.336
  366.1 1.6 convert_element_type.344
  367.7 2.0 convert_element_type.339
  (244 shorter events, 51.2 us)
Async XLA Ops:
  7.2 90.8 %copy-start = (bf16[1,2,8,16,512]{4,3,2,1,0:T(8,128)(2,1)S(1)}, bf16[1,2,8,16,512]{4,3,2,1,0:T(8,128)(2,1)}, u32[]{:S(2)}) copy-start(bf16[1,2,8,16,512]{4,3,2,1,0:T(8,128)(2,1)} %param.7) | copy-start | bytes 786436
  7.2 64.7 %copy-start.35 = (s32[1,2,8,16]{3,2,1,0:T(8,128)S(1)}, s32[1,2,8,16]{3,2,1,0:T(8,128)}, u32[]{:S(2)}) copy-start(s32[1,2,8,16]{3,2,1,0:T(8,128)} %param.8) | copy-start | bytes 3076
  7.2 70.6 %copy-start.33 = (bf16[1,128,512]{2,1,0:T(8,128)(2,1)S(1)}, bf16[1,128,512]{2,1,0:T(8,128)(2,1)}, u32[]{:S(2)}) copy-start(bf16[1,128,512]{2,1,0:T(8,128)(2,1)} %param.11) | copy-start | bytes 393220
  7.2 31.9 %all-gather.7.cloned.1.call-start = ((), (), s32[]{:S(2)}) async-start(), calls=%async_computation.11 | async-start | bytes 1310720 | tf_op jit(solution)/shard_map/all_gather | solution.py:158
  7.9 80.5 %copy-start.44 = (bf16[1,128]{1,0:T(2,128)(2,1)S(1)}, bf16[1,128]{1,0:T(2,128)(2,1)}, u32[]{:S(2)}) copy-start(bf16[1,128]{1,0:T(2,128)(2,1)} %param.12) | copy-start | bytes 772
  7.9 63.9 %all-gather.11.cloned.1.call-start = ((), (), s32[]{:S(2)}) async-start(), calls=%async_computation.13 | async-start | bytes 1966080 | tf_op jit(solution)/shard_map/all_gather | solution.py:159
  8.7 89.3 %copy-start.28 = (bf16[1,2,8,16,512]{4,3,2,1,0:T(8,128)(2,1)S(1)}, bf16[1,2,8,16,512]{4,3,2,1,0:T(8,128)(2,1)}, u32[]{:S(2)}) copy-start(bf16[1,2,8,16,512]{4,3,2,1,0:T(8,128)(2,1)} %param.13) | copy-start | bytes 786436
  8.7 89.8 %all-gather.9.cloned.1.call-start = ((), (), s32[]{:S(2)}) async-start(), calls=%async_computation.12 | async-start | bytes 3145728 | tf_op jit(solution)/shard_map/all_gather | solution.py:174
  39.1 61.2 %all-gather.13.cloned.1.call-start = ((), (), s32[]{:S(2)}) async-start(), calls=%async_computation.14 | async-start | bytes 4718592 | tf_op jit(solution)/shard_map/all_gather | solution.py:175
  71.8 38.5 %all-gather.15.cloned.1.call-start = ((), (), s32[]{:S(2)}) async-start(), calls=%async_computation.15 | async-start | bytes 1572864 | tf_op jit(solution)/shard_map/all_gather | solution.py:176
  71.9 26.2 %collective-permute-start.3 = (s32[2,4,16]{2,1,0:T(4,128)S(1)}, s32[2,4,16]{2,1,0:T(4,128)S(1)}, u32[]{:S(2)}, u32[]{:S(2)}) collective-permute-start(s32[2,4,16]{2,1,0:T(4,128)S(1)} %get-tuple-element.46), channel_id=1, source_target_pairs={{1,0},{2,1},{3,2},{5,4},{6,5},{7,6},{9,8},{10,9},{11,10},{13,12},{... | collective-permute-start | bytes 1544 | tf_op jit(solution)/shard_map/ppermute | solution.py:23
  73.2 24.9 %collective-permute-start.2 = (s32[2,4,16]{2,1,0:T(4,128)S(1)}, s32[2,4,16]{2,1,0:T(4,128)S(1)}, u32[]{:S(2)}, u32[]{:S(2)}) collective-permute-start(s32[2,4,16]{2,1,0:T(4,128)S(1)} %get-tuple-element.47), channel_id=1, source_target_pairs={{0,1},{1,2},{2,3},{4,5},{5,6},{6,7},{8,9},{9,10},{10,11},{12,13},{... | collective-permute-start | bytes 1544 | tf_op jit(solution)/shard_map/ppermute | solution.py:22
  98.0 4.2 %copy-start.41 = (f32[1,1,512]{2,1,0:T(1,128)}, f32[1,1,512]{2,1,0:T(1,128)S(1)}, u32[]{:S(2)}) copy-start(f32[1,1,512]{2,1,0:T(1,128)S(1)} %get-tuple-element.49) | copy-start | bytes 6148
  98.0 4.2 %copy-start.13 = (bf16[8,16,512]{2,1,0:T(8,128)(2,1)}, bf16[8,16,512]{2,1,0:T(8,128)(2,1)S(1)}, u32[]{:S(2)}) copy-start(bf16[8,16,512]{2,1,0:T(8,128)(2,1)S(1)} %dynamic-slice_bitcast_fusion) | copy-start | bytes 393220
  98.0 12.3 %copy-start.16 = (bf16[1,1,8,16,512]{4,3,2,1,0:T(8,128)(2,1)}, bf16[1,1,8,16,512]{4,3,2,1,0:T(8,128)(2,1)S(1)}, u32[]{:S(2)}) copy-start(bf16[1,1,8,16,512]{4,3,2,1,0:T(8,128)(2,1)S(1)} %constant_dynamic-slice_fusion) | copy-start | bytes 393220
  98.5 16.0 %copy-start.25 = (pred[128,256]{1,0:T(8,128)(4,1)}, pred[128,256]{1,0:T(8,128)(4,1)S(1)}, u32[]{:S(2)}) copy-start(pred[128,256]{1,0:T(8,128)(4,1)S(1)} %or_and_fusion) | copy-start | bytes 98308
  100.1 17.2 %copy-start.6 = (f32[8,16,512]{2,1,0:T(8,128)}, f32[8,16,512]{2,1,0:T(8,128)S(1)}, u32[]{:S(2)}) copy-start(f32[8,16,512]{2,1,0:T(8,128)S(1)} %get-tuple-element.53) | copy-start | bytes 786436
  102.3 10.2 %collective-permute-start = (bf16[4,16,1024]{2,1,0:T(8,128)(2,1)S(1)}, bf16[4,16,1024]{2,1,0:T(8,128)(2,1)S(1)}, u32[]{:S(2)}, u32[]{:S(2)}) collective-permute-start(bf16[4,16,1024]{2,1,0:T(8,128)(2,1)S(1)} %get-tuple-element.35), channel_id=1, source_target_pairs={{0,1},{1,2},{2,3},{4,5},{5,6},{6,7},{8,9},{9,10},{10,11},{12,13},{... | collective-permute-start | bytes 393224 | tf_op jit(solution)/shard_map/ppermute | solution.py:22
  105.7 7.2 %collective-permute-start.1 = (bf16[4,16,1024]{2,1,0:T(8,128)(2,1)S(1)}, bf16[4,16,1024]{2,1,0:T(8,128)(2,1)S(1)}, u32[]{:S(2)}, u32[]{:S(2)}) collective-permute-start(bf16[4,16,1024]{2,1,0:T(8,128)(2,1)S(1)} %get-tuple-element.36), channel_id=1, source_target_pairs={{1,0},{2,1},{3,2},{5,4},{6,5},{7,6},{9,8},{10,9},{11,10},{13,12},{... | collective-permute-start | bytes 393224 | tf_op jit(solution)/shard_map/ppermute | solution.py:23
  117.3 3.3 copy-start.45
  118.7 3.0 copy-start.9
  120.4 4.5 %copy-start.4 = (f32[8,16,512]{2,1,0:T(8,128)}, f32[8,16,512]{2,1,0:T(8,128)S(1)}, u32[]{:S(2)}) copy-start(f32[8,16,512]{2,1,0:T(8,128)S(1)} %get-tuple-element.57) | copy-start | bytes 786436
  125.8 6.9 %collective-permute-start.4 = (bf16[4,16,1024]{2,1,0:T(8,128)(2,1)}, bf16[4,16,1024]{2,1,0:T(8,128)(2,1)S(1)}, u32[]{:S(2)}, u32[]{:S(2)}) collective-permute-start(bf16[4,16,1024]{2,1,0:T(8,128)(2,1)} %get-tuple-element.33), channel_id=1, source_target_pairs={{0,1},{1,2},{2,3},{4,5},{5,6},{6,7},{8,9},{9,10},{10,11},{12,13},{... | collective-permute-start | bytes 393224 | tf_op jit(solution)/shard_map/ppermute | solution.py:22
  129.2 7.3 %collective-permute-start.5 = (bf16[4,16,1024]{2,1,0:T(8,128)(2,1)S(1)}, bf16[4,16,1024]{2,1,0:T(8,128)(2,1)S(1)}, u32[]{:S(2)}, u32[]{:S(2)}) collective-permute-start(bf16[4,16,1024]{2,1,0:T(8,128)(2,1)S(1)} %get-tuple-element.34), channel_id=1, source_target_pairs={{1,0},{2,1},{3,2},{5,4},{6,5},{7,6},{9,8},{10,9},{11,10},{13,12},{... | collective-permute-start | bytes 393224 | tf_op jit(solution)/shard_map/ppermute | solution.py:23
  148.3 7.5 %copy-start.2 = (bf16[1,128,8,64]{3,2,1,0:T(8,128)(2,1)}, bf16[1,128,8,64]{3,2,1,0:T(8,128)(2,1)S(1)}, u32[]{:S(2)}) copy-start(bf16[1,128,8,64]{3,2,1,0:T(8,128)(2,1)S(1)} %copy.58) | copy-start | bytes 393220
  149.3 46.7 %all-to-all-start.5 = ((bf16[2,1,8,16,512]{4,3,2,1,0:T(8,128)(2,1)}), bf16[2,1,8,16,512]{4,3,2,1,0:T(8,128)(2,1)}, u32[]{:S(2)}, u32[]{:S(2)}) async-start(bf16[2,1,8,16,512]{4,3,2,1,0:T(8,128)(2,1)} %pad_maximum_fusion.13), calls=%async_computation.7 | async-start | bytes 524288 | tf_op jit(solution)/shard_map/all_to_all | solution.py:241
  153.4 76.8 %reduce-scatter.11.cloned.1.call-start = ((), (), s32[]{:S(2)}) async-start(), calls=%async_computation.18 | async-start | bytes 655360 | tf_op jit(solution)/shard_map/reduce_scatter | solution.py:273
  160.0 12.0 %copy-start.5 = (f32[8,16,512]{2,1,0:T(8,128)S(1)}, f32[8,16,512]{2,1,0:T(8,128)}, u32[]{:S(2)}) copy-start(f32[8,16,512]{2,1,0:T(8,128)} %copy-done.4) | copy-start | bytes 786436
  160.0 12.0 %copy-start.39 = (f32[8,16]{1,0:T(8,128)S(1)}, f32[8,16]{1,0:T(8,128)}, u32[]{:S(2)}) copy-start(f32[8,16]{1,0:T(8,128)} %copy-done.38) | copy-start | bytes 1540
  160.0 12.0 %copy-start.43 = (f32[1,1,512]{2,1,0:T(1,128)S(1)}, f32[1,1,512]{2,1,0:T(1,128)}, u32[]{:S(2)}) copy-start(f32[1,1,512]{2,1,0:T(1,128)} %get-tuple-element.48) | copy-start | bytes 6148
  161.1 6.7 %collective-permute-start.6 = (bf16[4,16,1024]{2,1,0:T(8,128)(2,1)S(1)}, bf16[4,16,1024]{2,1,0:T(8,128)(2,1)S(1)}, u32[]{:S(2)}, u32[]{:S(2)}) collective-permute-start(bf16[4,16,1024]{2,1,0:T(8,128)(2,1)S(1)} %get-tuple-element.29), channel_id=1, source_target_pairs={{0,1},{1,2},{2,3},{4,5},{5,6},{6,7},{8,9},{9,10},{10,11},{12,13},{... | collective-permute-start | bytes 393224 | tf_op jit(solution)/shard_map/ppermute | solution.py:22
  164.4 7.5 %collective-permute-start.7 = (bf16[4,16,1024]{2,1,0:T(8,128)(2,1)S(1)}, bf16[4,16,1024]{2,1,0:T(8,128)(2,1)S(1)}, u32[]{:S(2)}, u32[]{:S(2)}) collective-permute-start(bf16[4,16,1024]{2,1,0:T(8,128)(2,1)S(1)} %get-tuple-element.30), channel_id=1, source_target_pairs={{1,0},{2,1},{3,2},{5,4},{6,5},{7,6},{9,8},{10,9},{11,10},{13,12},{... | collective-permute-start | bytes 393224 | tf_op jit(solution)/shard_map/ppermute | solution.py:23
  167.0 7.4 %copy-start.29 = (bf16[1,2,8,16,512]{4,3,2,1,0:T(8,128)(2,1)S(1)}, bf16[1,2,8,16,512]{4,3,2,1,0:T(8,128)(2,1)}, u32[]{:S(2)}) copy-start(bf16[1,2,8,16,512]{4,3,2,1,0:T(8,128)(2,1)} %param.13) | copy-start | bytes 786436
  182.4 11.1 %copy-start.7 = (f32[8,16,512]{2,1,0:T(8,128)S(1)}, f32[8,16,512]{2,1,0:T(8,128)}, u32[]{:S(2)}) copy-start(f32[8,16,512]{2,1,0:T(8,128)} %copy-done.6) | copy-start | bytes 786436
  182.4 11.1 %copy-start.37 = (f32[8,16]{1,0:T(8,128)S(1)}, f32[8,16]{1,0:T(8,128)}, u32[]{:S(2)}) copy-start(f32[8,16]{1,0:T(8,128)} %copy-done.36) | copy-start | bytes 1540
  182.4 11.1 %copy-start.42 = (f32[1,1,512]{2,1,0:T(1,128)S(1)}, f32[1,1,512]{2,1,0:T(1,128)}, u32[]{:S(2)}) copy-start(f32[1,1,512]{2,1,0:T(1,128)} %copy-done.41) | copy-start | bytes 6148
  183.2 5.9 %collective-permute-start.8 = (bf16[4,16,1024]{2,1,0:T(8,128)(2,1)S(1)}, bf16[4,16,1024]{2,1,0:T(8,128)(2,1)S(1)}, u32[]{:S(2)}, u32[]{:S(2)}) collective-permute-start(bf16[4,16,1024]{2,1,0:T(8,128)(2,1)S(1)} %get-tuple-element.23), channel_id=1, source_target_pairs={{0,1},{1,2},{2,3},{4,5},{5,6},{6,7},{8,9},{9,10},{10,11},{12,13},{... | collective-permute-start | bytes 393224 | tf_op jit(solution)/shard_map/ppermute | solution.py:22
  186.6 6.9 %collective-permute-start.9 = (bf16[4,16,1024]{2,1,0:T(8,128)(2,1)S(1)}, bf16[4,16,1024]{2,1,0:T(8,128)(2,1)S(1)}, u32[]{:S(2)}, u32[]{:S(2)}) collective-permute-start(bf16[4,16,1024]{2,1,0:T(8,128)(2,1)S(1)} %get-tuple-element.24), channel_id=1, source_target_pairs={{1,0},{2,1},{3,2},{5,4},{6,5},{7,6},{9,8},{10,9},{11,10},{13,12},{... | collective-permute-start | bytes 393224 | tf_op jit(solution)/shard_map/ppermute | solution.py:23
  187.9 7.8 %copy-start.32 = (bf16[8,16,1024]{2,1,0:T(8,128)(2,1)S(1)}, bf16[8,16,1024]{2,1,0:T(8,128)(2,1)}, u32[]{:S(2)}) copy-start(bf16[8,16,1024]{2,1,0:T(8,128)(2,1)} %copy-done.31) | copy-start | bytes 786436
  203.0 5.2 %all-to-all-start.1 = ((bf16[2,1,8,16,1024]{4,3,2,1,0:T(8,128)(2,1)}), bf16[2,1,8,16,1024]{4,3,2,1,0:T(8,128)(2,1)S(1)}, u32[]{:S(2)}, u32[]{:S(2)}) async-start(bf16[2,1,8,16,1024]{4,3,2,1,0:T(8,128)(2,1)} %pad_maximum_fusion.1), calls=%async_computation.1 | async-start | bytes 1048576 | tf_op jit(solution)/shard_map/all_to_all | solution.py:237
  206.5 49.9 %reduce-scatter.7.cloned.1.call-start = ((), (), s32[]{:S(2)}) async-start(), calls=%async_computation.16 | async-start | bytes 1310720 | tf_op jit(solution)/shard_map/reduce_scatter | solution.py:267
  214.4 5.0 %all-to-all-start.3 = ((bf16[2,1,8,16,512]{4,3,2,1,0:T(8,128)(2,1)}), bf16[2,1,8,16,512]{4,3,2,1,0:T(8,128)(2,1)S(1)}, u32[]{:S(2)}, u32[]{:S(2)}) async-start(bf16[2,1,8,16,512]{4,3,2,1,0:T(8,128)(2,1)} %pad_maximum_fusion.12), calls=%async_computation.4 | async-start | bytes 524288 | tf_op jit(solution)/shard_map/all_to_all | solution.py:239
  217.8 72.7 %reduce-scatter.9.cloned.1.call-start = ((), (), s32[]{:S(2)}) async-start(), calls=%async_computation.17 | async-start | bytes 1966080 | tf_op jit(solution)/shard_map/reduce_scatter | solution.py:270
  224.4 2.9 copy-start.1
  227.3 90.7 %reduce-scatter.13.cloned.1.call-start = ((), (), s32[]{:S(2)}) async-start(), calls=%async_computation.19 | async-start | bytes 163840
  228.8 61.8 %copy-start.3 = (bf16[1,128,8,64]{3,2,1,0:T(8,128)(2,1)S(1)}, bf16[1,128,8,64]{3,2,1,0:T(8,128)(2,1)}, u32[]{:S(2)}) copy-start(bf16[1,128,8,64]{3,2,1,0:T(8,128)(2,1)} %copy-done.2) | copy-start | bytes 393220
  228.8 62.0 %copy-start.12 = (bf16[2,512,512]{2,1,0:T(8,128)(2,1)S(1)}, bf16[2,512,512]{2,1,0:T(8,128)(2,1)}, u32[]{:S(2)}) copy-start(bf16[2,512,512]{2,1,0:T(8,128)(2,1)} %all-gather.15.cloned.1.call-done) | copy-start | bytes 3145732
  230.2 134.1 %all-reduce.11.cloned.1.call-start = ((), (), s32[]{:S(2)}) async-start(), calls=%async_computation.20 | async-start | bytes 1572864 | tf_op jit(solution)/shard_map/psum | solution.py:281
  (22 other events, 38.6 us)
Sparse Core Ops, SparseCore 0:
  9.9 29.2 all-gather.6
  40.9 30.8 all-gather.10
  73.4 10.5 all-gather.8
  85.4 13.2 all-gather.12
  100.1 10.1 all-gather.14
  202.2 23.2 reduce-scatter.10
  228.3 27.9 reduce-scatter.6
  259.3 31.1 reduce-scatter.8
  293.8 24.1 reduce-scatter.12
  320.4 43.7 all-reduce.10
where the time goes:
time: 379 us; the launch traced here: 377 us
  waiting for transfers between devices  203 us (54%)
  blocking collectives  47.4 us (13%)
  starting transfers between devices  36.4 us (10%)
  matrix products  32 us (8%)
  local copies, waits for them, and re-layouts  23.7 us (6%)
  other arithmetic  18.8 us (5%)
  between operations  15.6 us (4%)
    reduce_scatter x1, waiting for transfers between devices, body(): lax.psum_scatter(grad_sums[1][None].astype(jnp.bfloat16), 'dp', scatter_d...  34.2 us
    psum x1, waiting for transfers between devices, body(): lax.psum(merge_part_sum.astype(jnp.bfloat16), 'band').astype(jnp.float32)  33.2 us
    all_gather x1, waiting for transfers between devices, body(): lax.all_gather(qkv_weight, 'dp', axis=1, tiled=True)  32.6 us
    all_gather x1, waiting for transfers between devices, body(): lax.all_gather(merge_weight, 'dp', axis=1, tiled=True)  30.4 us
    reduce_scatter x1, waiting for transfers between devices, body(): lax.psum_scatter(grad_sums[0][None].astype(jnp.bfloat16), 'dp', scatter_d...  26.1 us
    unnamed x11, waiting for transfers between devices  24.5 us
    ppermute x5, starting transfers between devices, padded(): before = lax.ppermute(last, axis, up)  18.1 us
    ppermute x5, waiting for transfers between devices, padded(): after = lax.ppermute(first, axis, down)  12.6 us
  transfers between devices with their start and end apart: 23, of which 16 were waited for; matrix products, arithmetic and copies ran while one was open for 10% of the time, Pallas kernels for 0%

commit v1 on v0

--- a/solution.py
+++ b/solution.py
@@ -10,6 +10,28 @@
 SW = 8
 EPSILON = 1e-05
 MASKED = -1e30
+
+
+def joined_along(blocks, dim):
+    blocks = jnp.moveaxis(blocks, 0, dim)
+    lengths = blocks.shape
+    return blocks.reshape(*lengths[:dim], lengths[dim] * lengths[dim + 1], *lengths[dim + 2 :])
+
+
+def grow_blocks(x, axis):
+    size = lax.axis_size(axis)
+    parts = x[None]
+    for level in range(size.bit_length() - 1):
+        distance = 1 << level
+        other = lax.ppermute(parts, axis, [(i, i ^ distance) for i in range(size)])
+        both = jnp.stack([parts, other])
+        upper = lax.axis_index(axis) >> level & 1
+        parts = jnp.where(upper == 0, both, both[::-1]).reshape(-1, *x.shape)
+    return parts
+
+
+def gather_by_bits(value, axis, dim):
+    return joined_along(grow_blocks(value, axis), dim)
 
 
 def padded(shard, sides, width):
@@ -155,7 +177,7 @@
 
 def body(fields, cell_mask, merge_weight, qkv_weight, out_weight, norm_gain, out_cotangent):
     merge_rows, qkv_rows, out_rows, gain_rows = (
-        lax.all_gather(merge_weight, "dp", axis=1, tiled=True),
+        gather_by_bits(merge_weight, "dp", 1),
         lax.all_gather(qkv_weight, "dp", axis=1, tiled=True),
         lax.all_gather(out_weight, "dp", axis=1, tiled=True),
         lax.all_gather(norm_gain, "dp", axis=1, tiled=True),

time: 379 us -> 354 us (0.934)
  waiting for transfers between devices: 203 us -> 172 us
  starting transfers between devices: 36.4 us -> 41.4 us
    all_gather x1 -> x0, waiting for transfers between devices: 30.4 us -> none  [body(): lax.all_gather(merge_weight, 'dp', axis=1, tiled=True)]
    all_gather x1, waiting for transfers between devices: 32.6 us -> 10.3 us  [body(): lax.all_gather(qkv_weight, 'dp', axis=1, tiled=True)]
    ppermute x0 -> x2, waiting for transfers between devices: none -> 22 us  [grow_blocks(): other = lax.ppermute(parts, axis, [(i, i ^ distance) for i in range(size)])]
    ppermute x0 -> x2, starting transfers between devices: none -> 4.87 us  [grow_blocks(): other = lax.ppermute(parts, axis, [(i, i ^ distance) for i in range(size)])]
    unnamed x11 -> x10, waiting for transfers between devices: 24.5 us -> 23.9 us
  transfers between devices with their start and end apart: 23 -> 24, of which waited for: 16 -> 17; matrix products, arithmetic and copies ran while one was open for 10% -> 12% of each run, Pallas kernels for 0% -> 0%
where the time goes in v1:
time: 354 us; the launch traced here: 353 us
  waiting for transfers between devices  172 us (49%)
  blocking collectives  47.4 us (13%)
  starting transfers between devices  41.4 us (12%)
  matrix products  32 us (9%)
  local copies, waits for them, and re-layouts  23.7 us (7%)
  other arithmetic  21.2 us (6%)
  between operations  15.3 us (4%)
    reduce_scatter x1, waiting for transfers between devices, body(): lax.psum_scatter(grad_sums[1][None].astype(jnp.bfloat16), 'dp', scatter_d...  34.1 us
    psum x1, waiting for transfers between devices, body(): lax.psum(merge_part_sum.astype(jnp.bfloat16), 'band').astype(jnp.float32)  33.4 us
    reduce_scatter x1, waiting for transfers between devices, body(): lax.psum_scatter(grad_sums[0][None].astype(jnp.bfloat16), 'dp', scatter_d...  25.9 us
    unnamed x10, waiting for transfers between devices  23.9 us
    ppermute x2, waiting for transfers between devices, grow_blocks(): other = lax.ppermute(parts, axis, [(i, i ^ distance) for i in range(size)])  22 us
    ppermute x5, starting transfers between devices, padded(): before = lax.ppermute(last, axis, up)  18.2 us
    ppermute x5, waiting for transfers between devices, padded(): after = lax.ppermute(first, axis, down)  12.5 us
    psum x1, blocking collectives, body(): lax.psum(gain_part_sum.astype(jnp.bfloat16), 'band').astype(jnp.float32)  11.7 us
  transfers between devices with their start and end apart: 24, of which 17 were waited for; matrix products, arithmetic and copies ran while one was open for 12% of the time, Pallas kernels for 0%

profile of v1, /device:TPU:0, one launch (start us, length us, event | category | flops | bytes accessed | tf_op | source)
XLA Modules:
  0.0 352.9 jit_solution(750922988344615636)
XLA Ops:
  8.0 3.0 collective-permute-start
  11.0 6.5 %collective-permute-done = bf16[1,1,256,512]{3,2,1,0:T(8,128)(2,1)S(1)} collective-permute-done((bf16[1,1,256,512]{3,2,1,0:T(8,128)(2,1)}, bf16[1,1,256,512]{3,2,1,0:T(8,128)(2,1)S(1)}, u32[]{:S(2)}, u32[]{:S(2)}) %collective-permute-start) | collective-permute-done | bytes 262176 | tf_op jit(solution)/shard_map/ppermute | solution.py:26
  18.6 1.8 collective-permute-start.1
  20.5 15.5 %collective-permute-done.1 = bf16[2,1,256,512]{3,2,0,1:T(8,128)(2,1)S(1)} collective-permute-done((bf16[2,1,256,512]{3,2,0,1:T(8,128)(2,1)S(1)}, bf16[2,1,256,512]{3,2,0,1:T(8,128)(2,1)S(1)}, u32[]{:S(2)}, u32[]{:S(2)}) %collective-permute-start.1) | collective-permute-done | bytes 524320 | tf_op jit(solution)/shard_map/ppermute | solution.py:26
  37.5 10.3 %all-gather.8.cloned.1.call-done = bf16[1,512,1536]{2,1,0:T(8,128)(2,1)} async-done(((bf16[1,128,1536]{2,1,0:T(8,128)(2,1)}), bf16[1,512,1536]{2,1,0:T(8,128)(2,1)}) %all-gather.8.cloned.1.call-update) | async-done | bytes 1572880 | tf_op jit(solution)/shard_map/all_gather | solution.py:181
  49.1 4.5 %collective-permute-start.4 = (s32[2,4,16]{2,1,0:T(4,128)S(1)}, s32[2,4,16]{2,1,0:T(4,128)S(1)}, u32[]{:S(2)}, u32[]{:S(2)}) collective-permute-start(s32[2,4,16]{2,1,0:T(4,128)S(1)} %get-tuple-element.49), channel_id=1, source_target_pairs={{0,1},{1,2},{2,3},{4,5},{5,6},{6,7},{8,9},{9,10},{10,11},{12,13},{... | collective-permute-start | bytes 1544 | tf_op jit(solution)/shard_map/ppermute | solution.py:44
  53.7 10.6 %all_gather.26 = bf16[1,512,512]{2,1,0:T(8,128)(2,1)} all-gather(bf16[1,128,512]{2,1,0:T(8,128)(2,1)S(1)} %copy-done.33), channel_id=1, replica_groups=mesh['dp'=4,'segment'=2,'band'=4] {'dp'}, dimensions={1}, use_global_device_ids=true | all-gather | bytes 655360 | tf_op jit(solution)/shard_map/all_gather | solution.py:182
  64.4 7.1 %all_gather.22 = bf16[1,512]{1,0:T(2,128)(2,1)S(1)} all-gather(bf16[1,128]{1,0:T(2,128)(2,1)S(1)} %copy-done.44), channel_id=1, replica_groups=mesh['dp'=4,'segment'=2,'band'=4] {'dp'}, dimensions={1}, use_global_device_ids=true | all-gather | bytes 1280 | tf_op jit(solution)/shard_map/all_gather | solution.py:183
  71.5 1.8 all-gather
  74.4 1.6 fusion.134
  76.3 1.8 convolution_convert_fusion.1
  78.2 3.4 collective-permute-start.2
  82.9 3.5 all-gather.12.cloned.1.call-done
  94.7 1.6 fusion.136
  101.7 3.5 collective-permute-start.6
  105.2 1.5 collective-permute-start.7
  108.7 3.8 %collective-permute-done.7 = bf16[4,16,1024]{2,1,0:T(8,128)(2,1)S(1)} collective-permute-done((bf16[4,16,1024]{2,1,0:T(8,128)(2,1)S(1)}, bf16[4,16,1024]{2,1,0:T(8,128)(2,1)S(1)}, u32[]{:S(2)}, u32[]{:S(2)}) %collective-permute-start.7) | collective-permute-done | bytes 131104 | tf_op jit(solution)/shard_map/ppermute | solution.py:45
  112.5 1.7 pad_maximum_fusion.6
  120.4 1.7 fusion.19
  122.1 1.6 fusion.28
  125.4 4.1 %all-to-all-start.5 = ((bf16[2,1,8,16,512]{4,3,2,1,0:T(8,128)(2,1)}), bf16[2,1,8,16,512]{4,3,2,1,0:T(8,128)(2,1)}, u32[]{:S(2)}, u32[]{:S(2)}) async-start(bf16[2,1,8,16,512]{4,3,2,1,0:T(8,128)(2,1)} %pad_maximum_fusion.15), calls=%async_computation.7 | async-start | bytes 524288 | tf_op jit(solution)/shard_map/all_to_all | solution.py:263
  132.7 1.8 copy.63
  134.6 1.5 reshape.692
  137.1 3.4 collective-permute-start.8
  140.5 1.5 collective-permute-start.9
  143.9 4.1 %collective-permute-done.9 = bf16[4,16,1024]{2,1,0:T(8,128)(2,1)S(1)} collective-permute-done((bf16[4,16,1024]{2,1,0:T(8,128)(2,1)S(1)}, bf16[4,16,1024]{2,1,0:T(8,128)(2,1)S(1)}, u32[]{:S(2)}, u32[]{:S(2)}) %collective-permute-start.9) | collective-permute-done | bytes 131104 | tf_op jit(solution)/shard_map/ppermute | solution.py:45
  148.1 2.3 fusion.127
  154.4 1.7 fusion.29
  159.3 3.4 collective-permute-start.10
  165.1 4.4 %collective-permute-done.11 = bf16[4,16,1024]{2,1,0:T(8,128)(2,1)S(1)} collective-permute-done((bf16[4,16,1024]{2,1,0:T(8,128)(2,1)S(1)}, bf16[4,16,1024]{2,1,0:T(8,128)(2,1)S(1)}, u32[]{:S(2)}, u32[]{:S(2)}) %collective-permute-start.11) | collective-permute-done | bytes 131104 | tf_op jit(solution)/shard_map/ppermute | solution.py:45
  169.6 2.2 fusion.126
  172.0 3.9 %all_to_all.28 = bf16[2,1,8,16,512]{4,3,2,1,0:T(8,128)(2,1)S(1)} all-to-all(bf16[2,1,8,16,512]{4,3,2,1,0:T(8,128)(2,1)S(1)} %pad_maximum_fusion.16), channel_id=1, replica_groups=mesh['dp'=4,'segment'=2,'band'=4] {'segment'}, dimensions={0} | all-to-all | bytes 524288 | tf_op jit(solution)/shard_map/all_to_all | solution.py:264
  176.0 2.1 fusion.10
  179.0 3.5 all-to-all-start.1
  182.6 1.6 all-to-all-done.1
  184.3 3.9 %all_to_all.29 = bf16[2,1,8,16,512]{4,3,2,1,0:T(8,128)(2,1)S(1)} all-to-all(bf16[2,1,8,16,512]{4,3,2,1,0:T(8,128)(2,1)S(1)} %pad_maximum_fusion.13), channel_id=1, replica_groups=mesh['dp'=4,'segment'=2,'band'=4] {'segment'}, dimensions={0} | all-to-all | bytes 524288 | tf_op jit(solution)/shard_map/all_to_all | solution.py:260
  190.5 3.4 all-to-all-start.3
  196.2 4.4 %all_to_all.30 = bf16[2,1,8,16,1536]{4,3,2,1,0:T(8,128)(2,1)S(1)} all-to-all(bf16[2,1,8,16,1536]{4,3,2,1,0:T(8,128)(2,1)S(1)} %pad_maximum_fusion.1), channel_id=1, replica_groups=mesh['dp'=4,'segment'=2,'band'=4] {'segment'}, dimensions={0} | all-to-all | bytes 1572864 | tf_op jit(solution)/shard_map/all_to_all | solution.py:262
  200.5 2.8 fusion.1
  206.3 25.9 %reduce-scatter.7.cloned.1.call-done = bf16[1,256,512]{2,1,0:T(8,128)(2,1)} async-done(((bf16[1,1024,512]{2,1,0:T(8,128)(2,1)}), bf16[1,256,512]{2,1,0:T(8,128)(2,1)}) %reduce-scatter.7.cloned.1.call-update) | async-done | bytes 262160 | tf_op jit(solution)/shard_map/reduce_scatter | solution.py:289
  232.3 34.1 %reduce-scatter.9.cloned.1.call-done = bf16[1,128,1536]{2,1,0:T(8,128)(2,1)} async-done(((bf16[1,512,1536]{2,1,0:T(8,128)(2,1)}), bf16[1,128,1536]{2,1,0:T(8,128)(2,1)}) %reduce-scatter.9.cloned.1.call-update) | async-done | bytes 393232 | tf_op jit(solution)/shard_map/reduce_scatter | solution.py:292
  266.9 3.9 %all_to_all.31 = bf16[2,1,8,16,512]{4,3,2,1,0:T(8,128)(2,1)S(1)} all-to-all(bf16[2,1,8,16,512]{4,3,2,1,0:T(8,128)(2,1)S(1)} %pad_maximum_fusion.12), channel_id=1, replica_groups=mesh['dp'=4,'segment'=2,'band'=4] {'segment'}, dimensions={0} | all-to-all | bytes 524288 | tf_op jit(solution)/shard_map/all_to_all | solution.py:258
  270.9 23.0 %reduce-scatter.13.cloned.1.call-done = bf16[128,1]{1,0:T(8,128)(2,1)} async-done(((bf16[512,1]{1,0:T(8,128)(2,1)}), bf16[128,1]{1,0:T(8,128)(2,1)}) %reduce-scatter.13.cloned.1.call-update) | async-done | bytes 272
  294.7 11.7 %psum.31 = bf16[1,128]{1,0:T(2,128)(2,1)S(1)} all-reduce(bf16[1,128]{1,0:T(2,128)(2,1)S(1)} %copy.77), channel_id=1, replica_groups=mesh['dp'=4,'segment'=2,'band'=4] {'band'}, use_global_device_ids=true, to_apply=%region_28.29 | all-reduce | flops 128 | bytes 512 | tf_op jit(solution)/shard_map/psum | solution.py:306
  306.9 33.4 %all-reduce.11.cloned.1.call-done = (bf16[1,256,512]{2,1,0:T(8,128)(2,1)}, bf16[1,128,1536]{2,1,0:T(8,128)(2,1)}, bf16[1,128,512]{2,1,0:T(8,128)(2,1)}) async-done(((bf16[1,256,512]{2,1,0:T(8,128)(2,1)}, bf16[1,128,1536]{2,1,0:T(8,128)(2,1)}, bf16[1,128,512]{2,1,0:T(8,128)(2,1)}), (bf16[1,256,512]{2,1,0:T(8,128)(2,1)}, bf16[1,128,1536]{2,1,0:T(8,128)(2,1)}, ...) | async-done | bytes 786448 | tf_op jit(solution)/shard_map/psum | solution.py:303
  340.3 1.8 convert_element_type.336
  342.1 1.6 convert_element_type.344
  343.7 2.0 convert_element_type.339
  (249 shorter events, 57.0 us)
Async XLA Ops:
  7.2 66.7 %copy-start = (bf16[1,2,8,16,512]{4,3,2,1,0:T(8,128)(2,1)S(1)}, bf16[1,2,8,16,512]{4,3,2,1,0:T(8,128)(2,1)}, u32[]{:S(2)}) copy-start(bf16[1,2,8,16,512]{4,3,2,1,0:T(8,128)(2,1)} %param.7) | copy-start | bytes 786436
  7.2 40.6 %all-gather.8.cloned.1.call-start = ((), (), s32[]{:S(2)}) async-start(), calls=%async_computation.12 | async-start | bytes 1966080 | tf_op jit(solution)/shard_map/all_gather | solution.py:181
  7.9 66.5 %all-gather.6.cloned.1.call-start = ((), (), s32[]{:S(2)}) async-start(), calls=%async_computation.11 | async-start | bytes 3145728 | tf_op jit(solution)/shard_map/all_gather | solution.py:196
  8.0 9.5 %collective-permute-start = (bf16[1,1,256,512]{3,2,1,0:T(8,128)(2,1)}, bf16[1,1,256,512]{3,2,1,0:T(8,128)(2,1)S(1)}, u32[]{:S(2)}, u32[]{:S(2)}) collective-permute-start(bf16[1,1,256,512]{3,2,1,0:T(8,128)(2,1)} %bitcast.262), channel_id=1, source_target_pairs={{0,8},{8,0},{16,24},{24,16},{1,9},{9,1},{17,25},{25,17},{2,10},{10... | collective-permute-start | bytes 786440 | tf_op jit(solution)/shard_map/ppermute | solution.py:26
  18.6 17.4 %collective-permute-start.1 = (bf16[2,1,256,512]{3,2,0,1:T(8,128)(2,1)S(1)}, bf16[2,1,256,512]{3,2,0,1:T(8,128)(2,1)S(1)}, u32[]{:S(2)}, u32[]{:S(2)}) collective-permute-start(bf16[2,1,256,512]{3,2,0,1:T(8,128)(2,1)S(1)} %get-tuple-element.34), channel_id=1, source_target_pairs={{0,16},{8,24},{16,0},{24,8},{1,17},{9,25},{17,1},{25,9},{2,18},{10... | collective-permute-start | bytes 1572872 | tf_op jit(solution)/shard_map/ppermute | solution.py:26
  36.1 11.7 %copy-start.35 = (s32[1,2,8,16]{3,2,1,0:T(8,128)S(1)}, s32[1,2,8,16]{3,2,1,0:T(8,128)}, u32[]{:S(2)}) copy-start(s32[1,2,8,16]{3,2,1,0:T(8,128)} %param.8) | copy-start | bytes 3076
  36.1 17.6 %copy-start.33 = (bf16[1,128,512]{2,1,0:T(8,128)(2,1)S(1)}, bf16[1,128,512]{2,1,0:T(8,128)(2,1)}, u32[]{:S(2)}) copy-start(bf16[1,128,512]{2,1,0:T(8,128)(2,1)} %param.11) | copy-start | bytes 393220
  37.4 27.0 %copy-start.44 = (bf16[1,128]{1,0:T(2,128)(2,1)S(1)}, bf16[1,128]{1,0:T(2,128)(2,1)}, u32[]{:S(2)}) copy-start(bf16[1,128]{1,0:T(2,128)(2,1)} %param.12) | copy-start | bytes 772
  37.4 36.5 %copy-start.28 = (bf16[1,2,8,16,512]{4,3,2,1,0:T(8,128)(2,1)S(1)}, bf16[1,2,8,16,512]{4,3,2,1,0:T(8,128)(2,1)}, u32[]{:S(2)}) copy-start(bf16[1,2,8,16,512]{4,3,2,1,0:T(8,128)(2,1)} %param.13) | copy-start | bytes 786436
  37.4 38.9 %all-gather.10.cloned.1.call-start = ((), (), s32[]{:S(2)}) async-start(), calls=%async_computation.13 | async-start | bytes 4718592 | tf_op jit(solution)/shard_map/all_gather | solution.py:197
  47.8 38.6 %all-gather.12.cloned.1.call-start = ((), (), s32[]{:S(2)}) async-start(), calls=%async_computation.14 | async-start | bytes 1572864 | tf_op jit(solution)/shard_map/all_gather | solution.py:198
  47.8 26.2 %collective-permute-start.5 = (s32[2,4,16]{2,1,0:T(4,128)S(1)}, s32[2,4,16]{2,1,0:T(4,128)S(1)}, u32[]{:S(2)}, u32[]{:S(2)}) collective-permute-start(s32[2,4,16]{2,1,0:T(4,128)S(1)} %get-tuple-element.48), channel_id=1, source_target_pairs={{1,0},{2,1},{3,2},{5,4},{6,5},{7,6},{9,8},{10,9},{11,10},{13,12},{... | collective-permute-start | bytes 1544 | tf_op jit(solution)/shard_map/ppermute | solution.py:45
  49.1 24.9 %collective-permute-start.4 = (s32[2,4,16]{2,1,0:T(4,128)S(1)}, s32[2,4,16]{2,1,0:T(4,128)S(1)}, u32[]{:S(2)}, u32[]{:S(2)}) collective-permute-start(s32[2,4,16]{2,1,0:T(4,128)S(1)} %get-tuple-element.49), channel_id=1, source_target_pairs={{0,1},{1,2},{2,3},{4,5},{5,6},{6,7},{8,9},{9,10},{10,11},{12,13},{... | collective-permute-start | bytes 1544 | tf_op jit(solution)/shard_map/ppermute | solution.py:44
  73.9 4.2 %copy-start.41 = (f32[1,1,512]{2,1,0:T(1,128)}, f32[1,1,512]{2,1,0:T(1,128)S(1)}, u32[]{:S(2)}) copy-start(f32[1,1,512]{2,1,0:T(1,128)S(1)} %get-tuple-element.51) | copy-start | bytes 6148
  73.9 4.2 %copy-start.13 = (bf16[8,16,512]{2,1,0:T(8,128)(2,1)}, bf16[8,16,512]{2,1,0:T(8,128)(2,1)S(1)}, u32[]{:S(2)}) copy-start(bf16[8,16,512]{2,1,0:T(8,128)(2,1)S(1)} %dynamic-slice_bitcast_fusion) | copy-start | bytes 393220
  74.0 12.4 %copy-start.16 = (bf16[1,1,8,16,512]{4,3,2,1,0:T(8,128)(2,1)}, bf16[1,1,8,16,512]{4,3,2,1,0:T(8,128)(2,1)S(1)}, u32[]{:S(2)}) copy-start(bf16[1,1,8,16,512]{4,3,2,1,0:T(8,128)(2,1)S(1)} %constant_dynamic-slice_fusion) | copy-start | bytes 393220
  74.4 16.1 %copy-start.25 = (pred[128,256]{1,0:T(8,128)(4,1)}, pred[128,256]{1,0:T(8,128)(4,1)S(1)}, u32[]{:S(2)}) copy-start(pred[128,256]{1,0:T(8,128)(4,1)S(1)} %or_and_fusion) | copy-start | bytes 98308
  76.1 17.2 %copy-start.6 = (f32[8,16,512]{2,1,0:T(8,128)}, f32[8,16,512]{2,1,0:T(8,128)S(1)}, u32[]{:S(2)}) copy-start(f32[8,16,512]{2,1,0:T(8,128)S(1)} %get-tuple-element.55) | copy-start | bytes 786436
  78.2 10.4 %collective-permute-start.2 = (bf16[4,16,1024]{2,1,0:T(8,128)(2,1)S(1)}, bf16[4,16,1024]{2,1,0:T(8,128)(2,1)S(1)}, u32[]{:S(2)}, u32[]{:S(2)}) collective-permute-start(bf16[4,16,1024]{2,1,0:T(8,128)(2,1)S(1)} %get-tuple-element.37), channel_id=1, source_target_pairs={{0,1},{1,2},{2,3},{4,5},{5,6},{6,7},{8,9},{9,10},{10,11},{12,13},{... | collective-permute-start | bytes 393224 | tf_op jit(solution)/shard_map/ppermute | solution.py:44
  81.6 7.2 %collective-permute-start.3 = (bf16[4,16,1024]{2,1,0:T(8,128)(2,1)S(1)}, bf16[4,16,1024]{2,1,0:T(8,128)(2,1)S(1)}, u32[]{:S(2)}, u32[]{:S(2)}) collective-permute-start(bf16[4,16,1024]{2,1,0:T(8,128)(2,1)S(1)} %get-tuple-element.38), channel_id=1, source_target_pairs={{1,0},{2,1},{3,2},{5,4},{6,5},{7,6},{9,8},{10,9},{11,10},{13,12},{... | collective-permute-start | bytes 393224 | tf_op jit(solution)/shard_map/ppermute | solution.py:45
  93.2 3.3 copy-start.45
  94.7 3.0 copy-start.9
  96.3 4.5 %copy-start.4 = (f32[8,16,512]{2,1,0:T(8,128)}, f32[8,16,512]{2,1,0:T(8,128)S(1)}, u32[]{:S(2)}) copy-start(f32[8,16,512]{2,1,0:T(8,128)S(1)} %get-tuple-element.59) | copy-start | bytes 786436
  101.7 7.0 %collective-permute-start.6 = (bf16[4,16,1024]{2,1,0:T(8,128)(2,1)}, bf16[4,16,1024]{2,1,0:T(8,128)(2,1)S(1)}, u32[]{:S(2)}, u32[]{:S(2)}) collective-permute-start(bf16[4,16,1024]{2,1,0:T(8,128)(2,1)} %get-tuple-element.35), channel_id=1, source_target_pairs={{0,1},{1,2},{2,3},{4,5},{5,6},{6,7},{8,9},{9,10},{10,11},{12,13},{... | collective-permute-start | bytes 393224 | tf_op jit(solution)/shard_map/ppermute | solution.py:44
  105.2 7.3 %collective-permute-start.7 = (bf16[4,16,1024]{2,1,0:T(8,128)(2,1)S(1)}, bf16[4,16,1024]{2,1,0:T(8,128)(2,1)S(1)}, u32[]{:S(2)}, u32[]{:S(2)}) collective-permute-start(bf16[4,16,1024]{2,1,0:T(8,128)(2,1)S(1)} %get-tuple-element.36), channel_id=1, source_target_pairs={{1,0},{2,1},{3,2},{5,4},{6,5},{7,6},{9,8},{10,9},{11,10},{13,12},{... | collective-permute-start | bytes 393224 | tf_op jit(solution)/shard_map/ppermute | solution.py:45
  124.4 7.5 %copy-start.2 = (bf16[1,128,8,64]{3,2,1,0:T(8,128)(2,1)}, bf16[1,128,8,64]{3,2,1,0:T(8,128)(2,1)S(1)}, u32[]{:S(2)}) copy-start(bf16[1,128,8,64]{3,2,1,0:T(8,128)(2,1)S(1)} %copy.58) | copy-start | bytes 393220
  125.4 46.7 %all-to-all-start.5 = ((bf16[2,1,8,16,512]{4,3,2,1,0:T(8,128)(2,1)}), bf16[2,1,8,16,512]{4,3,2,1,0:T(8,128)(2,1)}, u32[]{:S(2)}, u32[]{:S(2)}) async-start(bf16[2,1,8,16,512]{4,3,2,1,0:T(8,128)(2,1)} %pad_maximum_fusion.15), calls=%async_computation.7 | async-start | bytes 524288 | tf_op jit(solution)/shard_map/all_to_all | solution.py:263
  129.5 76.8 %reduce-scatter.11.cloned.1.call-start = ((), (), s32[]{:S(2)}) async-start(), calls=%async_computation.17 | async-start | bytes 655360 | tf_op jit(solution)/shard_map/reduce_scatter | solution.py:295
  136.1 12.0 %copy-start.5 = (f32[8,16,512]{2,1,0:T(8,128)S(1)}, f32[8,16,512]{2,1,0:T(8,128)}, u32[]{:S(2)}) copy-start(f32[8,16,512]{2,1,0:T(8,128)} %copy-done.4) | copy-start | bytes 786436
  136.1 12.0 %copy-start.39 = (f32[8,16]{1,0:T(8,128)S(1)}, f32[8,16]{1,0:T(8,128)}, u32[]{:S(2)}) copy-start(f32[8,16]{1,0:T(8,128)} %copy-done.38) | copy-start | bytes 1540
  136.1 12.0 %copy-start.43 = (f32[1,1,512]{2,1,0:T(1,128)S(1)}, f32[1,1,512]{2,1,0:T(1,128)}, u32[]{:S(2)}) copy-start(f32[1,1,512]{2,1,0:T(1,128)} %get-tuple-element.50) | copy-start | bytes 6148
  137.1 6.7 %collective-permute-start.8 = (bf16[4,16,1024]{2,1,0:T(8,128)(2,1)S(1)}, bf16[4,16,1024]{2,1,0:T(8,128)(2,1)S(1)}, u32[]{:S(2)}, u32[]{:S(2)}) collective-permute-start(bf16[4,16,1024]{2,1,0:T(8,128)(2,1)S(1)} %get-tuple-element.29), channel_id=1, source_target_pairs={{0,1},{1,2},{2,3},{4,5},{5,6},{6,7},{8,9},{9,10},{10,11},{12,13},{... | collective-permute-start | bytes 393224 | tf_op jit(solution)/shard_map/ppermute | solution.py:44
  140.5 7.5 %collective-permute-start.9 = (bf16[4,16,1024]{2,1,0:T(8,128)(2,1)S(1)}, bf16[4,16,1024]{2,1,0:T(8,128)(2,1)S(1)}, u32[]{:S(2)}, u32[]{:S(2)}) collective-permute-start(bf16[4,16,1024]{2,1,0:T(8,128)(2,1)S(1)} %get-tuple-element.30), channel_id=1, source_target_pairs={{1,0},{2,1},{3,2},{5,4},{6,5},{7,6},{9,8},{10,9},{11,10},{13,12},{... | collective-permute-start | bytes 393224 | tf_op jit(solution)/shard_map/ppermute | solution.py:45
  143.1 7.4 %copy-start.29 = (bf16[1,2,8,16,512]{4,3,2,1,0:T(8,128)(2,1)S(1)}, bf16[1,2,8,16,512]{4,3,2,1,0:T(8,128)(2,1)}, u32[]{:S(2)}) copy-start(bf16[1,2,8,16,512]{4,3,2,1,0:T(8,128)(2,1)} %param.13) | copy-start | bytes 786436
  158.5 11.1 %copy-start.7 = (f32[8,16,512]{2,1,0:T(8,128)S(1)}, f32[8,16,512]{2,1,0:T(8,128)}, u32[]{:S(2)}) copy-start(f32[8,16,512]{2,1,0:T(8,128)} %copy-done.6) | copy-start | bytes 786436
  158.5 11.1 %copy-start.37 = (f32[8,16]{1,0:T(8,128)S(1)}, f32[8,16]{1,0:T(8,128)}, u32[]{:S(2)}) copy-start(f32[8,16]{1,0:T(8,128)} %copy-done.36) | copy-start | bytes 1540
  158.5 11.1 %copy-start.42 = (f32[1,1,512]{2,1,0:T(1,128)S(1)}, f32[1,1,512]{2,1,0:T(1,128)}, u32[]{:S(2)}) copy-start(f32[1,1,512]{2,1,0:T(1,128)} %copy-done.41) | copy-start | bytes 6148
  159.3 5.9 %collective-permute-start.10 = (bf16[4,16,1024]{2,1,0:T(8,128)(2,1)S(1)}, bf16[4,16,1024]{2,1,0:T(8,128)(2,1)S(1)}, u32[]{:S(2)}, u32[]{:S(2)}) collective-permute-start(bf16[4,16,1024]{2,1,0:T(8,128)(2,1)S(1)} %get-tuple-element.23), channel_id=1, source_target_pairs={{0,1},{1,2},{2,3},{4,5},{5,6},{6,7},{8,9},{9,10},{10,11},{12,13},{... | collective-permute-start | bytes 393224 | tf_op jit(solution)/shard_map/ppermute | solution.py:44
  162.6 6.9 %collective-permute-start.11 = (bf16[4,16,1024]{2,1,0:T(8,128)(2,1)S(1)}, bf16[4,16,1024]{2,1,0:T(8,128)(2,1)S(1)}, u32[]{:S(2)}, u32[]{:S(2)}) collective-permute-start(bf16[4,16,1024]{2,1,0:T(8,128)(2,1)S(1)} %get-tuple-element.24), channel_id=1, source_target_pairs={{1,0},{2,1},{3,2},{5,4},{6,5},{7,6},{9,8},{10,9},{11,10},{13,12},{... | collective-permute-start | bytes 393224 | tf_op jit(solution)/shard_map/ppermute | solution.py:45
  164.0 7.8 %copy-start.32 = (bf16[8,16,1024]{2,1,0:T(8,128)(2,1)S(1)}, bf16[8,16,1024]{2,1,0:T(8,128)(2,1)}, u32[]{:S(2)}) copy-start(bf16[8,16,1024]{2,1,0:T(8,128)(2,1)} %copy-done.31) | copy-start | bytes 786436
  179.0 5.2 %all-to-all-start.1 = ((bf16[2,1,8,16,1024]{4,3,2,1,0:T(8,128)(2,1)}), bf16[2,1,8,16,1024]{4,3,2,1,0:T(8,128)(2,1)S(1)}, u32[]{:S(2)}, u32[]{:S(2)}) async-start(bf16[2,1,8,16,1024]{4,3,2,1,0:T(8,128)(2,1)} %pad_maximum_fusion.3), calls=%async_computation.1 | async-start | bytes 1048576 | tf_op jit(solution)/shard_map/all_to_all | solution.py:259
  182.5 49.7 %reduce-scatter.7.cloned.1.call-start = ((), (), s32[]{:S(2)}) async-start(), calls=%async_computation.15 | async-start | bytes 1310720 | tf_op jit(solution)/shard_map/reduce_scatter | solution.py:289
  190.5 5.0 %all-to-all-start.3 = ((bf16[2,1,8,16,512]{4,3,2,1,0:T(8,128)(2,1)}), bf16[2,1,8,16,512]{4,3,2,1,0:T(8,128)(2,1)S(1)}, u32[]{:S(2)}, u32[]{:S(2)}) async-start(bf16[2,1,8,16,512]{4,3,2,1,0:T(8,128)(2,1)} %pad_maximum_fusion.14), calls=%async_computation.4 | async-start | bytes 524288 | tf_op jit(solution)/shard_map/all_to_all | solution.py:261
  193.9 72.5 %reduce-scatter.9.cloned.1.call-start = ((), (), s32[]{:S(2)}) async-start(), calls=%async_computation.16 | async-start | bytes 1966080 | tf_op jit(solution)/shard_map/reduce_scatter | solution.py:292
  203.4 90.5 %reduce-scatter.13.cloned.1.call-start = ((), (), s32[]{:S(2)}) async-start(), calls=%async_computation.18 | async-start | bytes 163840
  204.8 61.6 %copy-start.3 = (bf16[1,128,8,64]{3,2,1,0:T(8,128)(2,1)S(1)}, bf16[1,128,8,64]{3,2,1,0:T(8,128)(2,1)}, u32[]{:S(2)}) copy-start(bf16[1,128,8,64]{3,2,1,0:T(8,128)(2,1)} %copy-done.2) | copy-start | bytes 393220
  204.8 61.8 %copy-start.12 = (bf16[2,512,512]{2,1,0:T(8,128)(2,1)S(1)}, bf16[2,512,512]{2,1,0:T(8,128)(2,1)}, u32[]{:S(2)}) copy-start(bf16[2,512,512]{2,1,0:T(8,128)(2,1)} %all-gather.12.cloned.1.call-done) | copy-start | bytes 3145732
  206.3 134.0 %all-reduce.11.cloned.1.call-start = ((), (), s32[]{:S(2)}) async-start(), calls=%async_computation.19 | async-start | bytes 1572864 | tf_op jit(solution)/shard_map/psum | solution.py:303
  (23 other events, 41.3 us)
Sparse Core Ops, SparseCore 0:
  9.8 37.8 all-gather.7
  49.3 10.5 all-gather.5
  61.4 13.2 all-gather.9
  76.2 10.1 all-gather.11
  178.2 23.2 reduce-scatter.10
  204.3 27.9 reduce-scatter.6
  235.2 31.0 reduce-scatter.8
  269.7 24.1 reduce-scatter.12
  296.5 43.7 all-reduce.10
